TPU v7x, 32 devices: a whole 2x2x4 slice. The times are simulated.
32 devices in a mesh: seq: 32 (over z, y, x, core).
Axes of the slice: x: 2, y: 2, z: 4, core: 2. Of those that a mesh axis runs over, the one named last changes fastest.
Arguments:
- hidden: bfloat16 [4096, 2048], P('seq'), may hold values from -6 to 6
- queries: bfloat16 [4096, 2048], P('seq'), may hold values from -6 to 6
- key_rows: bfloat16 [4096, 512], P('seq'), may hold values from -6 to 6
- grad_out: bfloat16 [4096, 2048], P('seq'), may hold values from -6 to 6
- master_value: float32 [2048, 512], P('seq'), may hold values from -0.125 to 0.125
- adam_first: float32 [2048, 512], P('seq'), may hold values from -12 to 12
- adam_second: float32 [2048, 512], P('seq'), may hold values from 1 to 100
Outputs:
- attention: bfloat16 [4096, 2048], P('seq')
- grad_queries: bfloat16 [4096, 2048], P('seq')
- grad_keys: bfloat16 [4096, 512], P('seq')
- grad_hidden: bfloat16 [4096, 2048], P('seq')
- new_master: float32 [2048, 512], P('seq')
- new_first: float32 [2048, 512], P('seq')
- new_second: float32 [2048, 512], P('seq')
All inputs are finite; a program needn't handle non-finite values.
Results may differ from a plain program's by a relative error of at most 0.02.
Values may be sent and summed in bfloat16 or wider, within the bound.
No kernel may reach another device: no remote copies, remote signals or barrier semaphores. Data moves between devices by JAX's collectives and lax.ppermute only.
A program may use at most 64 MiB of HBM per device.

v0:
```python
import math
import jax
import jax.numpy as jnp
from jax import lax
from jax.sharding import PartitionSpec as P

HQ = 16
HK = 4
DH = 128
WINDOW = 512
OPT_STEP = 10
beta_first = 0.9
beta_second = 0.95
learning = 0.001
decay_rate = 0.1
epsilon = 1e-08


def passed_along(block, axis, distance):
    devices = range(lax.axis_size(axis))
    route = [(i - distance, i) for i in devices if i - distance in devices]
    return lax.ppermute(block, axis, route)


def attend_block(query_blk, grad_blk, key_win, value_win, allowed):
    ratio = HQ // HK
    scale = 1.0 / math.sqrt(DH)
    count = query_blk.shape[0]
    out_parts, dq_parts, dk_parts, dv_parts = ([], [], [], [])
    for group in range(HK):
        low = group * ratio * DH
        high = (group + 1) * ratio * DH
        query_group = query_blk[:, low:high].reshape(count, ratio, DH)
        grad_group = grad_blk[:, low:high].reshape(count, ratio, DH)
        key_group = key_win[:, group * DH : (group + 1) * DH]
        value_group = value_win[:, group * DH : (group + 1) * DH]
        scores = (
            jnp.einsum("trd,sd->trs", query_group, key_group, preferred_element_type=jnp.float32)
            * scale
        )
        scores = jnp.where(allowed[:, None, :], scores, -jnp.inf)
        top = jnp.max(scores, axis=2, keepdims=True)
        expd = jnp.exp(scores - top)
        probs = expd / jnp.sum(expd, axis=2, keepdims=True)
        probs_low = probs.astype(jnp.bfloat16)
        out_group = jnp.einsum(
            "trs,sd->trd", probs_low, value_group, preferred_element_type=jnp.float32
        ).astype(jnp.bfloat16)
        delta = jnp.sum(
            grad_group.astype(jnp.float32) * out_group.astype(jnp.float32), axis=2, keepdims=True
        )
        dprob = jnp.einsum(
            "trd,sd->trs", grad_group, value_group, preferred_element_type=jnp.float32
        )
        dscore = (probs * (dprob - delta)).astype(jnp.bfloat16)
        dq_group = (
            jnp.einsum("trs,sd->trd", dscore, key_group, preferred_element_type=jnp.float32) * scale
        ).astype(jnp.bfloat16)
        dk_group = (
            jnp.einsum("trs,trd->sd", dscore, query_group, preferred_element_type=jnp.float32)
            * scale
        )
        dv_group = jnp.einsum(
            "trs,trd->sd", probs_low, grad_group, preferred_element_type=jnp.float32
        )
        out_parts.append(out_group.reshape(count, ratio * DH))
        dq_parts.append(dq_group.reshape(count, ratio * DH))
        dk_parts.append(dk_group)
        dv_parts.append(dv_group)
    return (
        jnp.concatenate(out_parts, 1),
        jnp.concatenate(dq_parts, 1),
        jnp.concatenate(dk_parts, 1),
        jnp.concatenate(dv_parts, 1),
    )


def shards(hidden, queries, key_rows, grad_out, master_value, adam_first, adam_second):
    tok_rows = hidden.shape[0]
    reach = WINDOW // tok_rows
    position = lax.axis_index("seq")
    weight_low = master_value.astype(jnp.bfloat16)
    weight_full = lax.all_gather(weight_low, "seq", axis=0, tiled=True)
    values = jnp.dot(hidden, weight_full, preferred_element_type=jnp.float32).astype(jnp.bfloat16)
    earlier = []
    for distance in range(1, reach + 1):
        earlier.append(passed_along((key_rows, values), "seq", distance))
    ordered = earlier[::-1]
    key_win = jnp.concatenate([entry[0] for entry in ordered] + [key_rows], 0)
    value_win = jnp.concatenate([entry[1] for entry in ordered] + [values], 0)
    span_rows = (reach + 1) * tok_rows
    key_index = jnp.arange(span_rows, dtype=jnp.int32)
    key_pos = position * tok_rows - WINDOW + key_index
    relative = jnp.arange(tok_rows, dtype=jnp.int32)[:, None] + WINDOW - key_index[None, :]
    allowed = (relative >= 0) & (relative < WINDOW) & (key_pos >= 0)[None, :]
    attention, grad_queries, dk_win, dv_win = attend_block(
        queries, grad_out, key_win, value_win, allowed
    )

    def partial_terms(distance):
        low = (reach - distance) * tok_rows
        return (dk_win[low : low + tok_rows], dv_win[low : low + tok_rows])

    key_total, value_total = partial_terms(0)
    for distance in range(1, reach + 1):
        arrived = passed_along(partial_terms(distance), "seq", -distance)
        key_total = key_total + arrived[0]
        value_total = value_total + arrived[1]
    grad_keys = key_total.astype(jnp.bfloat16)
    d_value = value_total.astype(jnp.bfloat16)
    grad_hidden = lax.dot_general(
        d_value, weight_full, (((1,), (1,)), ((), ())), preferred_element_type=jnp.float32
    ).astype(jnp.bfloat16)
    grad_weight = lax.psum_scatter(
        lax.dot_general(
            hidden, d_value, (((0,), (0,)), ((), ())), preferred_element_type=jnp.float32
        ),
        "seq",
        scatter_dimension=0,
        tiled=True,
    )
    new_first = beta_first * adam_first + (1.0 - beta_first) * grad_weight
    new_second = beta_second * adam_second + (1.0 - beta_second) * grad_weight * grad_weight
    first_hat = new_first / (1.0 - beta_first**OPT_STEP)
    second_hat = new_second / (1.0 - beta_second**OPT_STEP)
    new_master = master_value - learning * (
        first_hat / (jnp.sqrt(second_hat) + epsilon) + decay_rate * master_value
    )
    return (attention, grad_queries, grad_keys, grad_hidden, new_master, new_first, new_second)


def solution(mesh):
    placed = (
        P("seq", None),
        P("seq", None),
        P("seq", None),
        P("seq", None),
        P("seq", None),
        P("seq", None),
        P("seq", None),
    )
    return jax.shard_map(
        shards,
        mesh=mesh,
        in_specs=placed,
        out_specs=(
            P("seq", None),
            P("seq", None),
            P("seq", None),
            P("seq", None),
            P("seq", None),
            P("seq", None),
            P("seq", None),
        ),
        check_vma=False,
    )
```

profile of v0, /device:TPU:6, one launch (start us, length us, event | category | flops | bytes accessed | tf_op | source)
XLA Modules:
  0.0 334.3 jit_solution(691577577510038583)
XLA Ops:
  7.2 3.5 %collective-permute-start.2 = (bf16[128,512]{1,0:T(8,128)(2,1)}, bf16[128,512]{1,0:T(8,128)(2,1)S(1)}, u32[]{:S(2)}, u32[]{:S(2)}) collective-permute-start(bf16[128,512]{1,0:T(8,128)(2,1)} %param.9), channel_id=1, source_target_pairs={{0,2},{1,3},{2,4},{3,5},{4,6},{5,7},{6,8},{7,9},{8,10},{9,11},{10,... | collective-permute-start | bytes 393224 | tf_op jit(solution)/shard_map/ppermute | solution.py:22
  10.8 2.6 collective-permute-start.1
  13.3 3.4 %collective-permute-start = (bf16[128,512]{1,0:T(8,128)(2,1)}, bf16[128,512]{1,0:T(8,128)(2,1)S(1)}, u32[]{:S(2)}, u32[]{:S(2)}) collective-permute-start(bf16[128,512]{1,0:T(8,128)(2,1)} %param.9), channel_id=1, source_target_pairs={{0,4},{1,5},{2,6},{3,7},{4,8},{5,9},{6,10},{7,11},{8,12},{9,13},{1... | collective-permute-start | bytes 393224 | tf_op jit(solution)/shard_map/ppermute | solution.py:22
  16.8 2.6 collective-permute-start.3
  25.7 2.7 fusion.76
  28.4 2.5 fusion.75
  30.9 2.5 fusion.77
  38.0 2.9 collective-permute-start.12
  45.2 2.9 collective-permute-start.13
  48.1 11.6 %collective-permute-done.15 = f32[128,512]{0,1:T(8,128)S(1)} collective-permute-done((f32[128,512]{0,1:T(8,128)S(1)}, f32[128,512]{0,1:T(8,128)S(1)}, u32[]{:S(2)}, u32[]{:S(2)}) %collective-permute-start.15) | collective-permute-done | bytes 262176 | tf_op jit(solution)/shard_map/ppermute | solution.py:22
  59.7 2.8 collective-permute-done.14
  62.5 2.9 collective-permute-done.13
  65.4 2.7 convolution_bitcast_fusion
  68.2 5.3 %copy.270 = f32[2048,512]{1,0:T(8,128)} copy(f32[2048,512]{0,1:T(8,128)} %convolution_bitcast_fusion) | data formatting | bytes 8388608
  73.6 127.5 %reduce-scatter.4.cloned.1.call-done = f32[64,512]{1,0:T(8,128)} async-done(((f32[2048,512]{1,0:T(8,128)}), f32[64,512]{1,0:T(8,128)}) %reduce-scatter.4.cloned.1.call-update) | async-done | bytes 131088 | tf_op jit(solution)/shard_map/reduce_scatter | solution.py:114
  203.0 67.2 %all-gather.2.cloned.1.call-done = bf16[2048,512]{1,0:T(8,128)(2,1)} async-done(((bf16[64,512]{1,0:T(8,128)(2,1)}), bf16[2048,512]{1,0:T(8,128)(2,1)}) %all-gather.2.cloned.1.call-update) | async-done | bytes 2097168 | tf_op jit(solution)/shard_map/all_gather | solution.py:83
  274.6 3.3 collective-permute-start.6
  277.9 4.1 %collective-permute-start.5 = (bf16[128,512]{1,0:T(8,128)(2,1)S(1)}, bf16[128,512]{1,0:T(8,128)(2,1)S(1)}, u32[]{:S(2)}, u32[]{:S(2)}) collective-permute-start(bf16[128,512]{1,0:T(8,128)(2,1)S(1)} %convolution_convert_fusion.5), channel_id=1, source_target_pairs={{0,3},{1,4},{2,5},{3,6},{4,7},{5,8},{6,9},{7,10},{8,11},{9,12},{10... | collective-permute-start | bytes 393224 | tf_op jit(solution)/shard_map/ppermute | solution.py:22
  282.0 2.7 collective-permute-start.4
  286.3 2.6 collective-permute-done.4
  299.2 2.7 collective-permute-start.8
  305.8 2.8 collective-permute-start.9
  311.1 9.3 %collective-permute-done.11 = f32[128,512]{0,1:T(8,128)S(1)} collective-permute-done((f32[128,512]{0,1:T(8,128)}, f32[128,512]{0,1:T(8,128)S(1)}, u32[]{:S(2)}, u32[]{:S(2)}) %collective-permute-start.11) | collective-permute-done | bytes 262176 | tf_op jit(solution)/shard_map/ppermute | solution.py:22
  320.4 2.8 collective-permute-done.10
  (144 shorter events, 43.7 us)
Async XLA Ops:
  7.2 58.3 %copy-start = (bf16[128,2048]{1,0:T(8,128)(2,1)S(1)}, bf16[128,2048]{1,0:T(8,128)(2,1)}, u32[]{:S(2)}) copy-start(bf16[128,2048]{1,0:T(8,128)(2,1)} %param.7) | copy-start | bytes 1572868
  7.2 13.4 %copy-start.22 = (bf16[128,2048]{1,0:T(8,128)(2,1)S(1)}, bf16[128,2048]{1,0:T(8,128)(2,1)}, u32[]{:S(2)}) copy-start(bf16[128,2048]{1,0:T(8,128)(2,1)} %param.10) | copy-start | bytes 1572868
  7.2 193.8 %reduce-scatter.4.cloned.1.call-start = ((), (), s32[]{:S(2)}) async-start(), calls=%async_computation.2 | async-start | bytes 4325376 | tf_op jit(solution)/shard_map/reduce_scatter | solution.py:114
  7.2 16.0 %collective-permute-start.2 = (bf16[128,512]{1,0:T(8,128)(2,1)}, bf16[128,512]{1,0:T(8,128)(2,1)S(1)}, u32[]{:S(2)}, u32[]{:S(2)}) collective-permute-start(bf16[128,512]{1,0:T(8,128)(2,1)} %param.9), channel_id=1, source_target_pairs={{0,2},{1,3},{2,4},{3,5},{4,6},{5,7},{6,8},{7,9},{8,10},{9,11},{10,... | collective-permute-start | bytes 393224 | tf_op jit(solution)/shard_map/ppermute | solution.py:22
  10.8 12.4 %collective-permute-start.1 = (bf16[128,512]{1,0:T(8,128)(2,1)}, bf16[128,512]{1,0:T(8,128)(2,1)S(1)}, u32[]{:S(2)}, u32[]{:S(2)}) collective-permute-start(bf16[128,512]{1,0:T(8,128)(2,1)} %param.9), channel_id=1, source_target_pairs={{0,3},{1,4},{2,5},{3,6},{4,7},{5,8},{6,9},{7,10},{8,11},{9,12},{10... | collective-permute-start | bytes 393224 | tf_op jit(solution)/shard_map/ppermute | solution.py:22
  13.3 9.8 %collective-permute-start = (bf16[128,512]{1,0:T(8,128)(2,1)}, bf16[128,512]{1,0:T(8,128)(2,1)S(1)}, u32[]{:S(2)}, u32[]{:S(2)}) collective-permute-start(bf16[128,512]{1,0:T(8,128)(2,1)} %param.9), channel_id=1, source_target_pairs={{0,4},{1,5},{2,6},{3,7},{4,8},{5,9},{6,10},{7,11},{8,12},{9,13},{1... | collective-permute-start | bytes 393224 | tf_op jit(solution)/shard_map/ppermute | solution.py:22
  16.8 6.5 %collective-permute-start.3 = (bf16[128,512]{1,0:T(8,128)(2,1)}, bf16[128,512]{1,0:T(8,128)(2,1)S(1)}, u32[]{:S(2)}, u32[]{:S(2)}) collective-permute-start(bf16[128,512]{1,0:T(8,128)(2,1)} %param.9), channel_id=1, source_target_pairs={{0,1},{1,2},{2,3},{3,4},{4,5},{5,6},{6,7},{7,8},{8,9},{9,10},{10,1... | collective-permute-start | bytes 393224 | tf_op jit(solution)/shard_map/ppermute | solution.py:22
  22.1 15.3 %copy-start.10 = (bf16[128,512]{0,1:T(8,128)(2,1)}, bf16[128,512]{0,1:T(8,128)(2,1)S(1)}, u32[]{:S(2)}) copy-start(bf16[128,512]{0,1:T(8,128)(2,1)S(1)} %copy.198) | copy-start | bytes 393220
  22.2 12.6 %copy-start.14 = (bf16[128,512]{0,1:T(8,128)(2,1)}, bf16[128,512]{0,1:T(8,128)(2,1)S(1)}, u32[]{:S(2)}) copy-start(bf16[128,512]{0,1:T(8,128)(2,1)S(1)} %copy.202) | copy-start | bytes 393220
  22.4 11.1 %copy-start.20 = (bf16[128,512]{0,1:T(8,128)(2,1)}, bf16[128,512]{0,1:T(8,128)(2,1)S(1)}, u32[]{:S(2)}) copy-start(bf16[128,512]{0,1:T(8,128)(2,1)S(1)} %copy.210) | copy-start | bytes 393220
  38.0 10.1 %collective-permute-start.12 = (f32[128,512]{0,1:T(8,128)S(1)}, f32[128,512]{0,1:T(8,128)S(1)}, u32[]{:S(2)}, u32[]{:S(2)}) collective-permute-start(f32[128,512]{0,1:T(8,128)S(1)} %get-tuple-element.38), channel_id=1, source_target_pairs={{1,0},{2,1},{3,2},{4,3},{5,4},{6,5},{7,6},{8,7},{9,8},{10,9},{11,1... | collective-permute-start | bytes 786440 | tf_op jit(solution)/shard_map/ppermute | solution.py:22
  40.9 18.8 %collective-permute-start.15 = (f32[128,512]{0,1:T(8,128)S(1)}, f32[128,512]{0,1:T(8,128)S(1)}, u32[]{:S(2)}, u32[]{:S(2)}) collective-permute-start(f32[128,512]{0,1:T(8,128)S(1)} %get-tuple-element.39), channel_id=1, source_target_pairs={{4,0},{5,1},{6,2},{7,3},{8,4},{9,5},{10,6},{11,7},{12,8},{13,9},{1... | collective-permute-start | bytes 786440 | tf_op jit(solution)/shard_map/ppermute | solution.py:22
  43.3 19.2 %collective-permute-start.14 = (f32[128,512]{0,1:T(8,128)S(1)}, f32[128,512]{0,1:T(8,128)S(1)}, u32[]{:S(2)}, u32[]{:S(2)}) collective-permute-start(f32[128,512]{0,1:T(8,128)S(1)} %get-tuple-element.40), channel_id=1, source_target_pairs={{3,0},{4,1},{5,2},{6,3},{7,4},{8,5},{9,6},{10,7},{11,8},{12,9},{13... | collective-permute-start | bytes 786440 | tf_op jit(solution)/shard_map/ppermute | solution.py:22
  45.2 20.1 %collective-permute-start.13 = (f32[128,512]{0,1:T(8,128)S(1)}, f32[128,512]{0,1:T(8,128)S(1)}, u32[]{:S(2)}, u32[]{:S(2)}) collective-permute-start(f32[128,512]{0,1:T(8,128)S(1)} %get-tuple-element.41), channel_id=1, source_target_pairs={{2,0},{3,1},{4,2},{5,3},{6,4},{7,5},{8,6},{9,7},{10,8},{11,9},{12,... | collective-permute-start | bytes 786440 | tf_op jit(solution)/shard_map/ppermute | solution.py:22
  73.5 196.7 %all-gather.2.cloned.1.call-start = ((), (), s32[]{:S(2)}) async-start(), calls=%async_computation.1 | async-start | bytes 2162688 | tf_op jit(solution)/shard_map/all_gather | solution.py:83
  270.2 14.4 %copy-start.1 = (bf16[2048,512]{1,0:T(8,128)(2,1)S(1)}, bf16[2048,512]{1,0:T(8,128)(2,1)}, u32[]{:S(2)}) copy-start(bf16[2048,512]{1,0:T(8,128)(2,1)} %all-gather.2.cloned.1.call-done) | copy-start | bytes 6291460
  272.4 16.5 %collective-permute-start.7 = (bf16[128,512]{1,0:T(8,128)(2,1)S(1)}, bf16[128,512]{1,0:T(8,128)(2,1)S(1)}, u32[]{:S(2)}, u32[]{:S(2)}) collective-permute-start(bf16[128,512]{1,0:T(8,128)(2,1)S(1)} %convolution_convert_fusion.5), channel_id=1, source_target_pairs={{0,1},{1,2},{2,3},{3,4},{4,5},{5,6},{6,7},{7,8},{8,9},{9,10},{10,1... | collective-permute-start | bytes 393224 | tf_op jit(solution)/shard_map/ppermute | solution.py:22
  274.6 14.3 %collective-permute-start.6 = (bf16[128,512]{1,0:T(8,128)(2,1)S(1)}, bf16[128,512]{1,0:T(8,128)(2,1)S(1)}, u32[]{:S(2)}, u32[]{:S(2)}) collective-permute-start(bf16[128,512]{1,0:T(8,128)(2,1)S(1)} %convolution_convert_fusion.5), channel_id=1, source_target_pairs={{0,2},{1,3},{2,4},{3,5},{4,6},{5,7},{6,8},{7,9},{8,10},{9,11},{10,... | collective-permute-start | bytes 393224 | tf_op jit(solution)/shard_map/ppermute | solution.py:22
  277.9 10.9 %collective-permute-start.5 = (bf16[128,512]{1,0:T(8,128)(2,1)S(1)}, bf16[128,512]{1,0:T(8,128)(2,1)S(1)}, u32[]{:S(2)}, u32[]{:S(2)}) collective-permute-start(bf16[128,512]{1,0:T(8,128)(2,1)S(1)} %convolution_convert_fusion.5), channel_id=1, source_target_pairs={{0,3},{1,4},{2,5},{3,6},{4,7},{5,8},{6,9},{7,10},{8,11},{9,12},{10... | collective-permute-start | bytes 393224 | tf_op jit(solution)/shard_map/ppermute | solution.py:22
  282.0 6.9 %collective-permute-start.4 = (bf16[128,512]{1,0:T(8,128)(2,1)S(1)}, bf16[128,512]{1,0:T(8,128)(2,1)S(1)}, u32[]{:S(2)}, u32[]{:S(2)}) collective-permute-start(bf16[128,512]{1,0:T(8,128)(2,1)S(1)} %convolution_convert_fusion.5), channel_id=1, source_target_pairs={{0,4},{1,5},{2,6},{3,7},{4,8},{5,9},{6,10},{7,11},{8,12},{9,13},{1... | collective-permute-start | bytes 393224 | tf_op jit(solution)/shard_map/ppermute | solution.py:22
  299.2 11.8 %collective-permute-start.8 = (f32[128,512]{0,1:T(8,128)}, f32[128,512]{0,1:T(8,128)S(1)}, u32[]{:S(2)}, u32[]{:S(2)}) collective-permute-start(f32[128,512]{0,1:T(8,128)} %get-tuple-element.42), channel_id=1, source_target_pairs={{1,0},{2,1},{3,2},{4,3},{5,4},{6,5},{7,6},{8,7},{9,8},{10,9},{11,1... | collective-permute-start | bytes 786440 | tf_op jit(solution)/shard_map/ppermute | solution.py:22
  302.0 18.4 %collective-permute-start.11 = (f32[128,512]{0,1:T(8,128)}, f32[128,512]{0,1:T(8,128)S(1)}, u32[]{:S(2)}, u32[]{:S(2)}) collective-permute-start(f32[128,512]{0,1:T(8,128)} %get-tuple-element.43), channel_id=1, source_target_pairs={{4,0},{5,1},{6,2},{7,3},{8,4},{9,5},{10,6},{11,7},{12,8},{13,9},{1... | collective-permute-start | bytes 786440 | tf_op jit(solution)/shard_map/ppermute | solution.py:22
  303.9 19.3 %collective-permute-start.10 = (f32[128,512]{0,1:T(8,128)}, f32[128,512]{0,1:T(8,128)}, u32[]{:S(2)}, u32[]{:S(2)}) collective-permute-start(f32[128,512]{0,1:T(8,128)} %get-tuple-element.44), channel_id=1, source_target_pairs={{3,0},{4,1},{5,2},{6,3},{7,4},{8,5},{9,6},{10,7},{11,8},{12,9},{13... | collective-permute-start | bytes 786440 | tf_op jit(solution)/shard_map/ppermute | solution.py:22
  305.8 19.8 %collective-permute-start.9 = (f32[128,512]{0,1:T(8,128)}, f32[128,512]{0,1:T(8,128)}, u32[]{:S(2)}, u32[]{:S(2)}) collective-permute-start(f32[128,512]{0,1:T(8,128)} %get-tuple-element.45), channel_id=1, source_target_pairs={{2,0},{3,1},{4,2},{5,3},{6,4},{7,5},{8,6},{9,7},{10,8},{11,9},{12,... | collective-permute-start | bytes 786440 | tf_op jit(solution)/shard_map/ppermute | solution.py:22
  (23 other events, 59.7 us)
Sparse Core Ops, SparseCore 0:
  73.6 127.3 reduce-scatter.3
  204.5 65.7 all-gather.1
where the time goes:
time: 335 us; the launch traced here: 334 us
  waiting for transfers between devices  229 us (68%)
  starting transfers between devices  43.9 us (13%)
  matrix products  23.7 us (7%)
  local copies, waits for them, and re-layouts  17.2 us (5%)
  between operations  14.8 us (4%)
  other arithmetic  5.69 us (2%)
    reduce_scatter x1, waiting for transfers between devices, shards(): lax.psum_scatter(lax.dot_general(hidden, d_value, (((0,), (0,)), ((), ())...  127 us
    all_gather x1, waiting for transfers between devices, shards(): weight_full = lax.all_gather(weight_low, 'seq', axis=0, tiled=True)  67.2 us
    ppermute x16, starting transfers between devices, passed_along(): return lax.ppermute(block, axis, route)  43.8 us
    ppermute x16, waiting for transfers between devices, passed_along(): return lax.ppermute(block, axis, route)  34.4 us
    unnamed x72, local copies, waits for them, and re-layouts  12.8 us
    sub x4, matrix products, attend_block(): expd = jnp.exp(scores - top)  9.17 us
  transfers between devices with their start and end apart: 18, of which 10 were waited for; matrix products, arithmetic and copies ran while one was open for 2% of the time, Pallas kernels for 0%

commit v1 on v0

--- a/solution.py
+++ b/solution.py
@@ -80,7 +80,14 @@
     reach = WINDOW // tok_rows
     position = lax.axis_index("seq")
     weight_low = master_value.astype(jnp.bfloat16)
-    weight_full = lax.all_gather(weight_low, "seq", axis=0, tiled=True)
+    ways, here = (lax.axis_size("seq"), lax.axis_index("seq"))
+    weight_full, reach_2 = (weight_low, 1)
+    while reach_2 < ways:
+        theirs = lax.ppermute(weight_full, "seq", [(d, d ^ reach_2) for d in range(ways)])
+        mine_first = jnp.concatenate([weight_full, theirs], axis=0)
+        theirs_first = jnp.concatenate([theirs, weight_full], axis=0)
+        weight_full = jnp.where(here & reach_2 == 0, mine_first, theirs_first)
+        reach_2 = 2 * reach_2
     values = jnp.dot(hidden, weight_full, preferred_element_type=jnp.float32).astype(jnp.bfloat16)
     earlier = []
     for distance in range(1, reach + 1):

time: 335 us -> 368 us (1.099); the launches traced: 334 us -> 363 us
  starting transfers between devices: 43.9 us -> 58.5 us
  other arithmetic: 5.69 us -> 12.3 us
    ppermute x0 -> x5, waiting for transfers between devices: none -> 71.4 us  [shards(): lax.ppermute(weight_full, 'seq', [(d, d ^ reach_2) for d in range(ways)])]
    all_gather x1 -> x0, waiting for transfers between devices: 67.2 us -> none  [shards(): weight_full = lax.all_gather(weight_low, 'seq', axis=0, tiled=True)]
    ppermute x0 -> x5, starting transfers between devices: none -> 16.1 us  [shards(): lax.ppermute(weight_full, 'seq', [(d, d ^ reach_2) for d in range(ways)])]
    select_n x0 -> x4, other arithmetic: none -> 6.06 us  [shards(): weight_full = jnp.where(here & reach_2 == 0, mine_first, theirs_first)]
    unnamed x72 -> x74, local copies, waits for them, and re-layouts: 12.8 us -> 13.5 us
  transfers between devices with their start and end apart: 18 -> 22, of which waited for: 10 -> 13; matrix products, arithmetic and copies ran while one was open for 2% -> 3% of each run, Pallas kernels for 0% -> 0%
where the time goes in v1:
time: 368 us; the launch traced here: 363 us
  waiting for transfers between devices  232 us (63%)
  starting transfers between devices  58.5 us (16%)
  matrix products  25.6 us (7%)
  local copies, waits for them, and re-layouts  20.3 us (6%)
  between operations  14.9 us (4%)
  other arithmetic  12.3 us (3%)
    reduce_scatter x1, waiting for transfers between devices, shards(): lax.psum_scatter(lax.dot_general(hidden, d_value, (((0,), (0,)), ((), ())...  130 us
    ppermute x5, waiting for transfers between devices, shards(): lax.ppermute(weight_full, 'seq', [(d, d ^ reach_2) for d in range(ways)])  71.4 us
    ppermute x16, starting transfers between devices, passed_along(): return lax.ppermute(block, axis, route)  42.4 us
    ppermute x16, waiting for transfers between devices, passed_along(): return lax.ppermute(block, axis, route)  31.1 us
    ppermute x5, starting transfers between devices, shards(): lax.ppermute(weight_full, 'seq', [(d, d ^ reach_2) for d in range(ways)])  16.1 us
    unnamed x74, local copies, waits for them, and re-layouts  13.5 us
    sub x4, matrix products, attend_block(): expd = jnp.exp(scores - top)  8.3 us
  transfers between devices with their start and end apart: 22, of which 13 were waited for; matrix products, arithmetic and copies ran while one was open for 3% of the time, Pallas kernels for 0%

profile of v1, /device:TPU:6, one launch (start us, length us, event | category | flops | bytes accessed | tf_op | source)
XLA Modules:
  0.0 363.5 jit_solution(18426510624071268028)
XLA Ops:
  7.2 3.6 collective-permute-start
  13.4 3.4 collective-permute-start.2
  26.5 2.7 fusion.78
  36.8 2.9 collective-permute-start.17
  39.7 3.3 collective-permute-start.18
  46.9 12.0 %collective-permute-done.18 = f32[128,512]{0,1:T(8,128)S(1)} collective-permute-done((f32[128,512]{0,1:T(8,128)S(1)}, f32[128,512]{0,1:T(8,128)S(1)}, u32[]{:S(2)}, u32[]{:S(2)}) %collective-permute-start.18) | collective-permute-done | bytes 262176 | tf_op jit(solution)/shard_map/ppermute | solution.py:22
  61.5 2.7 collective-permute-done.20
  64.9 2.7 convolution_bitcast_fusion
  67.6 5.3 %copy.270 = f32[2048,512]{1,0:T(8,128)} copy(f32[2048,512]{0,1:T(8,128)} %convolution_bitcast_fusion) | data formatting | bytes 8388608
  73.0 129.5 %reduce-scatter.4.cloned.1.call-done = f32[64,512]{1,0:T(8,128)} async-done(((f32[2048,512]{1,0:T(8,128)}), f32[64,512]{1,0:T(8,128)}) %reduce-scatter.4.cloned.1.call-update) | async-done | bytes 131088 | tf_op jit(solution)/shard_map/reduce_scatter | solution.py:121
  205.7 5.5 %collective-permute-start.5 = (bf16[128,512]{1,0:T(8,128)(2,1)S(1)}, bf16[128,512]{1,0:T(8,128)(2,1)}, u32[]{:S(2)}, u32[]{:S(2)}) collective-permute-start(bf16[128,512]{1,0:T(8,128)(2,1)S(1)} %maximum_select_fusion.6), channel_id=1, source_target_pairs={{0,2},{1,3},{2,0},{3,1},{4,6},{5,7},{6,4},{7,5},{8,10},{9,11},{10,... | collective-permute-start | bytes 393224 | tf_op jit(solution)/shard_map/ppermute | solution.py:86
  211.2 3.9 %collective-permute-done.5 = bf16[128,512]{1,0:T(8,128)(2,1)} collective-permute-done((bf16[128,512]{1,0:T(8,128)(2,1)S(1)}, bf16[128,512]{1,0:T(8,128)(2,1)}, u32[]{:S(2)}, u32[]{:S(2)}) %collective-permute-start.5) | collective-permute-done | bytes 131104 | tf_op jit(solution)/shard_map/ppermute | solution.py:86
  216.3 10.5 %collective-permute-start.6 = (bf16[256,512]{1,0:T(8,128)(2,1)S(1)}, bf16[256,512]{1,0:T(8,128)(2,1)}, u32[]{:S(2)}, u32[]{:S(2)}) collective-permute-start(bf16[256,512]{1,0:T(8,128)(2,1)S(1)} %maximum_select_fusion.5), channel_id=1, source_target_pairs={{0,4},{1,5},{2,6},{3,7},{4,0},{5,1},{6,2},{7,3},{8,12},{9,13},{10,... | collective-permute-start | bytes 786440 | tf_op jit(solution)/shard_map/ppermute | solution.py:86
  226.8 6.2 %collective-permute-done.6 = bf16[256,512]{1,0:T(8,128)(2,1)} collective-permute-done((bf16[256,512]{1,0:T(8,128)(2,1)S(1)}, bf16[256,512]{1,0:T(8,128)(2,1)}, u32[]{:S(2)}, u32[]{:S(2)}) %collective-permute-start.6) | collective-permute-done | bytes 262176 | tf_op jit(solution)/shard_map/ppermute | solution.py:86
  234.9 13.1 %collective-permute-done.7 = bf16[512,512]{1,0:T(8,128)(2,1)} collective-permute-done((bf16[512,512]{1,0:T(8,128)(2,1)}, bf16[512,512]{1,0:T(8,128)(2,1)}, u32[]{:S(2)}, u32[]{:S(2)}) %collective-permute-start.7) | collective-permute-done | bytes 524320 | tf_op jit(solution)/shard_map/ppermute | solution.py:86
  248.1 2.9 maximum_select_fusion.1
  251.0 46.9 %collective-permute-done.8 = bf16[1024,512]{1,0:T(8,128)(2,1)} collective-permute-done((bf16[1024,512]{1,0:T(8,128)(2,1)}, bf16[1024,512]{1,0:T(8,128)(2,1)}, u32[]{:S(2)}, u32[]{:S(2)}) %collective-permute-start.8) | collective-permute-done | bytes 1048608 | tf_op jit(solution)/shard_map/ppermute | solution.py:86
  297.9 2.8 fusion.40
  306.5 4.4 %collective-permute-start.12 = (bf16[128,512]{1,0:T(8,128)(2,1)S(1)}, bf16[128,512]{1,0:T(8,128)(2,1)S(1)}, u32[]{:S(2)}, u32[]{:S(2)}) collective-permute-start(bf16[128,512]{1,0:T(8,128)(2,1)S(1)} %fusion.40), channel_id=1, source_target_pairs={{0,1},{1,2},{2,3},{3,4},{4,5},{5,6},{6,7},{7,8},{8,9},{9,10},{10,1... | collective-permute-start | bytes 393224 | tf_op jit(solution)/shard_map/ppermute | solution.py:22
  310.9 3.8 %convolution_convert_fusion = bf16[128,2048]{1,0:T(8,128)(2,1)} fusion(bf16[128,512]{0,1:T(8,128)(2,1)S(1)} %copy-done.25, bf16[1024,512]{1,0:T(8,128)(2,1)} %collective-permute-done.8, bf16[1024,512]{1,0:T(8,128)(2,1)} %maximum_select_fusion.1, pred[]{:T(512)S(6)} %eq.15), kind=kOutput, calls=%fused_computation.5 | convolution fusion | flops 278134784 | bytes 2752513 | tf_op jit(solution)/shard_map/dot_general | solution.py:118
  328.8 4.2 %collective-permute-start.14 = (f32[128,512]{0,1:T(8,128)}, f32[128,512]{0,1:T(8,128)S(1)}, u32[]{:S(2)}, u32[]{:S(2)}) collective-permute-start(f32[128,512]{0,1:T(8,128)} %get-tuple-element.45), channel_id=1, source_target_pairs={{2,0},{3,1},{4,2},{5,3},{6,4},{7,5},{8,6},{9,7},{10,8},{11,9},{12,... | collective-permute-start | bytes 786440 | tf_op jit(solution)/shard_map/ppermute | solution.py:22
  341.1 8.4 %collective-permute-done.14 = f32[128,512]{0,1:T(8,128)S(1)} collective-permute-done((f32[128,512]{0,1:T(8,128)}, f32[128,512]{0,1:T(8,128)S(1)}, u32[]{:S(2)}, u32[]{:S(2)}) %collective-permute-start.14) | collective-permute-done | bytes 262176 | tf_op jit(solution)/shard_map/ppermute | solution.py:22
  349.5 2.6 collective-permute-done.15
  352.1 2.7 collective-permute-done.16
  (157 shorter events, 62.3 us)
Async XLA Ops:
  7.2 195.3 %reduce-scatter.4.cloned.1.call-start = ((), (), s32[]{:S(2)}) async-start(), calls=%async_computation.1 | async-start | bytes 4325376 | tf_op jit(solution)/shard_map/reduce_scatter | solution.py:121
  7.2 15.9 %collective-permute-start = (bf16[128,512]{1,0:T(8,128)(2,1)}, bf16[128,512]{1,0:T(8,128)(2,1)S(1)}, u32[]{:S(2)}, u32[]{:S(2)}) collective-permute-start(bf16[128,512]{1,0:T(8,128)(2,1)} %param.9), channel_id=1, source_target_pairs={{0,4},{1,5},{2,6},{3,7},{4,8},{5,9},{6,10},{7,11},{8,12},{9,13},{1... | collective-permute-start | bytes 393224 | tf_op jit(solution)/shard_map/ppermute | solution.py:22
  10.8 12.4 %collective-permute-start.1 = (bf16[128,512]{1,0:T(8,128)(2,1)}, bf16[128,512]{1,0:T(8,128)(2,1)S(1)}, u32[]{:S(2)}, u32[]{:S(2)}) collective-permute-start(bf16[128,512]{1,0:T(8,128)(2,1)} %param.9), channel_id=1, source_target_pairs={{0,3},{1,4},{2,5},{3,6},{4,7},{5,8},{6,9},{7,10},{8,11},{9,12},{10... | collective-permute-start | bytes 393224 | tf_op jit(solution)/shard_map/ppermute | solution.py:22
  13.4 9.8 %collective-permute-start.2 = (bf16[128,512]{1,0:T(8,128)(2,1)}, bf16[128,512]{1,0:T(8,128)(2,1)S(1)}, u32[]{:S(2)}, u32[]{:S(2)}) collective-permute-start(bf16[128,512]{1,0:T(8,128)(2,1)} %param.9), channel_id=1, source_target_pairs={{0,2},{1,3},{2,4},{3,5},{4,6},{5,7},{6,8},{7,9},{8,10},{9,11},{10,... | collective-permute-start | bytes 393224 | tf_op jit(solution)/shard_map/ppermute | solution.py:22
  16.8 6.5 %collective-permute-start.3 = (bf16[128,512]{1,0:T(8,128)(2,1)}, bf16[128,512]{1,0:T(8,128)(2,1)S(1)}, u32[]{:S(2)}, u32[]{:S(2)}) collective-permute-start(bf16[128,512]{1,0:T(8,128)(2,1)} %param.9), channel_id=1, source_target_pairs={{0,1},{1,2},{2,3},{3,4},{4,5},{5,6},{6,7},{7,8},{8,9},{9,10},{10,1... | collective-permute-start | bytes 393224 | tf_op jit(solution)/shard_map/ppermute | solution.py:22
  36.8 10.1 %collective-permute-start.17 = (f32[128,512]{0,1:T(8,128)S(1)}, f32[128,512]{0,1:T(8,128)S(1)}, u32[]{:S(2)}, u32[]{:S(2)}) collective-permute-start(f32[128,512]{0,1:T(8,128)S(1)} %get-tuple-element.38), channel_id=1, source_target_pairs={{1,0},{2,1},{3,2},{4,3},{5,4},{6,5},{7,6},{8,7},{9,8},{10,9},{11,1... | collective-permute-start | bytes 786440 | tf_op jit(solution)/shard_map/ppermute | solution.py:22
  39.7 19.3 %collective-permute-start.18 = (f32[128,512]{0,1:T(8,128)S(1)}, f32[128,512]{0,1:T(8,128)S(1)}, u32[]{:S(2)}, u32[]{:S(2)}) collective-permute-start(f32[128,512]{0,1:T(8,128)S(1)} %get-tuple-element.41), channel_id=1, source_target_pairs={{2,0},{3,1},{4,2},{5,3},{6,4},{7,5},{8,6},{9,7},{10,8},{11,9},{12,... | collective-permute-start | bytes 786440 | tf_op jit(solution)/shard_map/ppermute | solution.py:22
  43.1 18.4 %collective-permute-start.19 = (f32[128,512]{0,1:T(8,128)S(1)}, f32[128,512]{0,1:T(8,128)S(1)}, u32[]{:S(2)}, u32[]{:S(2)}) collective-permute-start(f32[128,512]{0,1:T(8,128)S(1)} %get-tuple-element.40), channel_id=1, source_target_pairs={{3,0},{4,1},{5,2},{6,3},{7,4},{8,5},{9,6},{10,7},{11,8},{12,9},{13... | collective-permute-start | bytes 786440 | tf_op jit(solution)/shard_map/ppermute | solution.py:22
  45.0 19.2 %collective-permute-start.20 = (f32[128,512]{0,1:T(8,128)S(1)}, f32[128,512]{0,1:T(8,128)S(1)}, u32[]{:S(2)}, u32[]{:S(2)}) collective-permute-start(f32[128,512]{0,1:T(8,128)S(1)} %get-tuple-element.39), channel_id=1, source_target_pairs={{4,0},{5,1},{6,2},{7,3},{8,4},{9,5},{10,6},{11,7},{12,8},{13,9},{1... | collective-permute-start | bytes 786440 | tf_op jit(solution)/shard_map/ppermute | solution.py:22
  73.0 129.6 %copy-start.26 = (f32[64,512]{1,0:T(8,128)S(1)}, f32[64,512]{1,0:T(8,128)}, u32[]{:S(2)}) copy-start(f32[64,512]{1,0:T(8,128)} %param.11) | copy-start | bytes 393220
  204.4 1.3 collective-permute-start.4
  205.7 9.5 %collective-permute-start.5 = (bf16[128,512]{1,0:T(8,128)(2,1)S(1)}, bf16[128,512]{1,0:T(8,128)(2,1)}, u32[]{:S(2)}, u32[]{:S(2)}) collective-permute-start(bf16[128,512]{1,0:T(8,128)(2,1)S(1)} %maximum_select_fusion.6), channel_id=1, source_target_pairs={{0,2},{1,3},{2,0},{3,1},{4,6},{5,7},{6,4},{7,5},{8,10},{9,11},{10,... | collective-permute-start | bytes 393224 | tf_op jit(solution)/shard_map/ppermute | solution.py:86
  216.3 16.7 %collective-permute-start.6 = (bf16[256,512]{1,0:T(8,128)(2,1)S(1)}, bf16[256,512]{1,0:T(8,128)(2,1)}, u32[]{:S(2)}, u32[]{:S(2)}) collective-permute-start(bf16[256,512]{1,0:T(8,128)(2,1)S(1)} %maximum_select_fusion.5), channel_id=1, source_target_pairs={{0,4},{1,5},{2,6},{3,7},{4,0},{5,1},{6,2},{7,3},{8,12},{9,13},{10,... | collective-permute-start | bytes 786440 | tf_op jit(solution)/shard_map/ppermute | solution.py:86
  234.9 13.1 %collective-permute-start.7 = (bf16[512,512]{1,0:T(8,128)(2,1)}, bf16[512,512]{1,0:T(8,128)(2,1)}, u32[]{:S(2)}, u32[]{:S(2)}) collective-permute-start(bf16[512,512]{1,0:T(8,128)(2,1)} %maximum_select_fusion.2), channel_id=1, source_target_pairs={{0,8},{1,9},{2,10},{3,11},{4,12},{5,13},{6,14},{7,15},{8,0},{9,1},... | collective-permute-start | bytes 1572872 | tf_op jit(solution)/shard_map/ppermute | solution.py:86
  251.0 46.9 %collective-permute-start.8 = (bf16[1024,512]{1,0:T(8,128)(2,1)}, bf16[1024,512]{1,0:T(8,128)(2,1)}, u32[]{:S(2)}, u32[]{:S(2)}) collective-permute-start(bf16[1024,512]{1,0:T(8,128)(2,1)} %maximum_select_fusion.1), channel_id=1, source_target_pairs={{0,16},{1,17},{2,18},{3,19},{4,20},{5,21},{6,22},{7,23},{8,24},{9,... | collective-permute-start | bytes 3145736 | tf_op jit(solution)/shard_map/ppermute | solution.py:86
  251.0 59.9 %copy-start.25 = (bf16[128,512]{0,1:T(8,128)(2,1)S(1)}, bf16[128,512]{0,1:T(8,128)(2,1)}, u32[]{:S(2)}) copy-start(bf16[128,512]{0,1:T(8,128)(2,1)} %copy-done.24) | copy-start | bytes 393220
  300.7 14.1 %collective-permute-start.9 = (bf16[128,512]{1,0:T(8,128)(2,1)S(1)}, bf16[128,512]{1,0:T(8,128)(2,1)S(1)}, u32[]{:S(2)}, u32[]{:S(2)}) collective-permute-start(bf16[128,512]{1,0:T(8,128)(2,1)S(1)} %fusion.40), channel_id=1, source_target_pairs={{0,4},{1,5},{2,6},{3,7},{4,8},{5,9},{6,10},{7,11},{8,12},{9,13},{1... | collective-permute-start | bytes 393224 | tf_op jit(solution)/shard_map/ppermute | solution.py:22
  302.6 12.1 %collective-permute-start.10 = (bf16[128,512]{1,0:T(8,128)(2,1)S(1)}, bf16[128,512]{1,0:T(8,128)(2,1)S(1)}, u32[]{:S(2)}, u32[]{:S(2)}) collective-permute-start(bf16[128,512]{1,0:T(8,128)(2,1)S(1)} %fusion.40), channel_id=1, source_target_pairs={{0,3},{1,4},{2,5},{3,6},{4,7},{5,8},{6,9},{7,10},{8,11},{9,12},{10... | collective-permute-start | bytes 393224 | tf_op jit(solution)/shard_map/ppermute | solution.py:22
  304.6 10.2 %collective-permute-start.11 = (bf16[128,512]{1,0:T(8,128)(2,1)S(1)}, bf16[128,512]{1,0:T(8,128)(2,1)S(1)}, u32[]{:S(2)}, u32[]{:S(2)}) collective-permute-start(bf16[128,512]{1,0:T(8,128)(2,1)S(1)} %fusion.40), channel_id=1, source_target_pairs={{0,2},{1,3},{2,4},{3,5},{4,6},{5,7},{6,8},{7,9},{8,10},{9,11},{10,... | collective-permute-start | bytes 393224 | tf_op jit(solution)/shard_map/ppermute | solution.py:22
  306.5 8.3 %collective-permute-start.12 = (bf16[128,512]{1,0:T(8,128)(2,1)S(1)}, bf16[128,512]{1,0:T(8,128)(2,1)S(1)}, u32[]{:S(2)}, u32[]{:S(2)}) collective-permute-start(bf16[128,512]{1,0:T(8,128)(2,1)S(1)} %fusion.40), channel_id=1, source_target_pairs={{0,1},{1,2},{2,3},{3,4},{4,5},{5,6},{6,7},{7,8},{8,9},{9,10},{10,1... | collective-permute-start | bytes 393224 | tf_op jit(solution)/shard_map/ppermute | solution.py:22
  326.9 14.2 %collective-permute-start.13 = (f32[128,512]{0,1:T(8,128)}, f32[128,512]{0,1:T(8,128)S(1)}, u32[]{:S(2)}, u32[]{:S(2)}) collective-permute-start(f32[128,512]{0,1:T(8,128)} %get-tuple-element.42), channel_id=1, source_target_pairs={{1,0},{2,1},{3,2},{4,3},{5,4},{6,5},{7,6},{8,7},{9,8},{10,9},{11,1... | collective-permute-start | bytes 786440 | tf_op jit(solution)/shard_map/ppermute | solution.py:22
  328.8 20.7 %collective-permute-start.14 = (f32[128,512]{0,1:T(8,128)}, f32[128,512]{0,1:T(8,128)S(1)}, u32[]{:S(2)}, u32[]{:S(2)}) collective-permute-start(f32[128,512]{0,1:T(8,128)} %get-tuple-element.45), channel_id=1, source_target_pairs={{2,0},{3,1},{4,2},{5,3},{6,4},{7,5},{8,6},{9,7},{10,8},{11,9},{12,... | collective-permute-start | bytes 786440 | tf_op jit(solution)/shard_map/ppermute | solution.py:22
  333.0 19.1 %collective-permute-start.15 = (f32[128,512]{0,1:T(8,128)}, f32[128,512]{0,1:T(8,128)}, u32[]{:S(2)}, u32[]{:S(2)}) collective-permute-start(f32[128,512]{0,1:T(8,128)} %get-tuple-element.44), channel_id=1, source_target_pairs={{3,0},{4,1},{5,2},{6,3},{7,4},{8,5},{9,6},{10,7},{11,8},{12,9},{13... | collective-permute-start | bytes 786440 | tf_op jit(solution)/shard_map/ppermute | solution.py:22
  334.9 19.8 %collective-permute-start.16 = (f32[128,512]{0,1:T(8,128)}, f32[128,512]{0,1:T(8,128)}, u32[]{:S(2)}, u32[]{:S(2)}) collective-permute-start(f32[128,512]{0,1:T(8,128)} %get-tuple-element.43), channel_id=1, source_target_pairs={{4,0},{5,1},{6,2},{7,3},{8,4},{9,5},{10,6},{11,7},{12,8},{13,9},{1... | collective-permute-start | bytes 786440 | tf_op jit(solution)/shard_map/ppermute | solution.py:22
  (28 other events, 143.5 us)
Sparse Core Ops, SparseCore 0:
  73.1 129.3 reduce-scatter.3
